TPU v7x, 256 devices: a whole 4x4x8 slice. The times are simulated.
256 devices in a mesh: node: 16 (over z_hi, y), slab: 16 (over x, z_lo, core).
Axes of the slice: x: 4, y: 4, z: 8 (z_hi: 4, z_lo: 2; z = z_hi * 2 + z_lo), core: 2. Of those that a mesh axis runs over, the one named last changes fastest.
Arguments:
- tensors: float32 [16, 128, 128, 128], P('node', 'slab'), may hold values from -0.375 to 0.375
- ops: float32 [8, 128, 128], replicated, as said below
- assign: int32 [16, 2], replicated, may hold values from 0 to 7
- parent: int32 [16], replicated, may hold values from 0 to 7, as said below
- env: float32 [128, 128], replicated, as said below
Outputs:
- gradient: float32 [16, 128, 128, 128], P('node', None, 'slab')
- energy: float32 [], replicated
Inputs may be any that keep to these rules, and one draw needn't show every extreme that they name: parent[0] = 0 and parent[1] = 0; for every level L from 2 to 4, each node of indices 2 ** (L - 1) to 2 ** L - 1 has its parent among indices 2 ** (L - 2) to 2 ** (L - 1) - 1, and each of those is the parent of exactly two of them. Every matrix ops[k] is symmetric. env is symmetric.
All inputs are finite; a program needn't handle non-finite values.
Results may differ from a plain program's by a relative error of at most 0.00012.
Values sent between devices are 32-bit elements; how exact they have to be, the bound alone decides.
A program may use at most 64 MiB of HBM per device.

v0:
```python
import jax
import jax.numpy as jnp
from jax import lax
from jax.sharding import PartitionSpec as P

LEVELS = 5
NODES = 16
HIGH = lax.Precision.HIGHEST


def links(parent):
    index = jnp.arange(NODES, dtype=jnp.int32)
    linked = (parent[None, :] == index[:, None]) & (index[None, :] >= 1)
    count = jnp.sum(linked.astype(jnp.int32), axis=1)
    left = jnp.min(jnp.where(linked, index[None, :], NODES), axis=1)
    right = jnp.max(jnp.where(linked, index[None, :], -1), axis=1)
    return (count, left, right)


def lookup(table, wanted):
    slots = jnp.arange(table.shape[0], dtype=jnp.int32)
    return jnp.sum(jnp.where(slots[None, :] == wanted[:, None], table[None, :], 0), axis=1)


def select_rows(onehot, stacked):
    return jnp.einsum("nm,mab->nab", onehot, stacked, precision=HIGH)


def per_device(tensors, ops, assign, parent, env):
    local_count = tensors.shape[0]
    width = tensors.shape[2]
    slab_rows = width // lax.axis_size("slab")
    node_ids = lax.axis_index("node") * local_count + jnp.arange(local_count, dtype=jnp.int32)
    slots = jnp.arange(NODES, dtype=jnp.int32)
    levels_all = jnp.zeros((NODES,), jnp.int32)
    for power in range(LEVELS - 1):
        levels_all = levels_all + (slots >= 2**power).astype(jnp.int32)
    my_level = lookup(levels_all, node_ids)
    count, left, right = links(parent)
    my_count = lookup(count, node_ids)
    my_left = lookup(left, node_ids)
    my_right = lookup(right, node_ids)
    table_ids = jnp.arange(ops.shape[0], dtype=jnp.int32)
    first_hot = (lookup(assign[:, 0], node_ids)[:, None] == table_ids[None, :]).astype(jnp.float32)
    second_hot = (lookup(assign[:, 1], node_ids)[:, None] == table_ids[None, :]).astype(jnp.float32)
    first_ops = jnp.einsum("nk,kab->nab", first_hot, ops, precision=HIGH)
    second_ops = jnp.einsum("nk,kab->nab", second_hot, ops, precision=HIGH)
    pair = jnp.einsum("nplr,nlm->npmr", tensors, first_ops, precision=HIGH)
    pair = jnp.einsum("npmr,nrs->npms", pair, second_ops, precision=HIGH)
    right_form = lax.all_to_all(
        tensors.transpose(0, 3, 1, 2), "slab", split_axis=1, concat_axis=2, tiled=True
    )
    left_form, pair_left = (
        lax.all_to_all(tensors, "slab", split_axis=2, concat_axis=1, tiled=True),
        lax.all_to_all(pair, "slab", split_axis=2, concat_axis=1, tiled=True),
    )
    zero_square = jnp.zeros((width, width), jnp.float32)
    left_store = jnp.zeros_like(right_form)
    right_store = jnp.zeros_like(left_form)
    left_ops = first_ops
    right_ops = second_ops
    onehot_left = (my_left[:, None] == slots[None, :]).astype(jnp.float32)
    onehot_right = (my_right[:, None] == slots[None, :]).astype(jnp.float32)
    energy = jnp.zeros((), jnp.float32)
    for level in range(LEVELS - 1, -1, -1):

        def climb(items, level=level):
            right_part, left_part, pair_part, left_op, right_op, left_old, right_old, node_level = (
                items
            )

            def climb_compute(unused):
                along_left = jnp.einsum("rpl,lm->rpm", right_part, left_op, precision=HIGH)
                along_right = (
                    jnp.einsum("plr,rs->pls", left_part, right_op, precision=HIGH) + pair_part
                )
                upper = jnp.einsum("rpm,rqm->pq", along_left, right_part, precision=HIGH)
                upper = upper + jnp.einsum("pls,qls->pq", along_right, left_part, precision=HIGH)
                return (along_left, along_right, upper)

            def climb_keep(unused):
                return (left_old, right_old, zero_square)

            return lax.cond(node_level == level, climb_compute, climb_keep, 0)

        left_store, right_store, partial_up = lax.map(
            climb,
            (
                right_form,
                left_form,
                pair_left,
                left_ops,
                right_ops,
                left_store,
                right_store,
                my_level,
            ),
        )
        up_rows = lax.psum_scatter(partial_up, "slab", scatter_dimension=1, tiled=True)
        if level > 0:
            every_rows = lax.all_gather(up_rows, "node", axis=0, tiled=True)
            left_rows = select_rows(onehot_left, every_rows)
            right_rows = select_rows(onehot_right, every_rows)
            left_full, right_full = (
                lax.all_gather(left_rows, "slab", axis=1, tiled=True),
                lax.all_gather(right_rows, "slab", axis=1, tiled=True),
            )
            ready = my_level == level - 1
            left_ops = jnp.where((ready & (my_count >= 1))[:, None, None], left_full, left_ops)
            right_ops = jnp.where((ready & (my_count >= 2))[:, None, None], right_full, right_ops)
        else:
            env_rows = lax.dynamic_slice_in_dim(
                env, lax.axis_index("slab") * slab_rows, slab_rows, 0
            )
            own = jnp.where(node_ids == 0, jnp.sum(up_rows * env_rows[None], axis=(1, 2)), 0.0)
            energy = lax.psum(jnp.sum(own), ("node", "slab"))
    down = jnp.where((node_ids == 0)[:, None, None], env[None], 0.0)
    parent_mine = lookup(parent, node_ids)
    is_left = lookup(left, parent_mine) == node_ids
    onehot_parent = (parent_mine[:, None] == slots[None, :]).astype(jnp.float32)
    for level in range(LEVELS - 1):

        def descend(items, level=level):
            right_part, left_part, down_now, node_level = items

            def descend_compute(unused):
                moved_r = jnp.einsum("pq,rql->rpl", down_now, right_part, precision=HIGH)
                down_left = jnp.einsum("rpl,rpm->lm", right_part, moved_r, precision=HIGH)
                moved_l = jnp.einsum("pq,qlr->plr", down_now, left_part, precision=HIGH)
                down_right = jnp.einsum("plr,pls->rs", left_part, moved_l, precision=HIGH)
                return (down_left, down_right)

            def descend_keep(unused):
                return (zero_square, zero_square)

            return lax.cond(node_level == level, descend_compute, descend_keep, 0)

        part_left, part_right = lax.map(descend, (right_form, left_form, down, my_level))
        rows_left, rows_right = (
            lax.psum_scatter(part_left, "slab", scatter_dimension=1, tiled=True),
            lax.psum_scatter(part_right, "slab", scatter_dimension=1, tiled=True),
        )
        every_left, every_right = (
            lax.all_gather(rows_left, "node", axis=0, tiled=True),
            lax.all_gather(rows_right, "node", axis=0, tiled=True),
        )
        from_left = select_rows(onehot_parent, every_left)
        from_right = select_rows(onehot_parent, every_right)
        mine = jnp.where(is_left[:, None, None], from_left, from_right)
        full_down = lax.all_gather(mine, "slab", axis=1, tiled=True)
        down = jnp.where((my_level == level + 1)[:, None, None], full_down, down)
    factor = width**0.75
    own_part = jnp.einsum("npq,nqlr->nplr", down, right_store, precision=HIGH)
    far_part = jnp.einsum("npq,nrql->nrpl", down, left_store, precision=HIGH)
    far_moved = lax.all_to_all(far_part, "slab", split_axis=3, concat_axis=1, tiled=True).transpose(
        0, 2, 3, 1
    )
    gradient = factor * (own_part + far_moved)
    return (gradient, energy)


def solution(mesh):
    return jax.shard_map(
        per_device,
        mesh=mesh,
        in_specs=(P("node", "slab", None, None), P(), P(), P(), P()),
        out_specs=(P("node", None, "slab", None), P()),
        check_vma=False,
    )
```

profile of v0, /device:TPU:1, one launch (start us, length us, event | category | flops | bytes accessed | tf_op | source)
XLA Modules:
  0.0 1453.6 jit_solution(2452833348320943357)
XLA Ops:
  8.6 1.4 fusion.39
  9.9 1.3 fusion.41
  12.4 1.1 copy.218
  13.5 7.2 all-to-all-start.2
  20.7 1.0 copy.197
  21.7 8.7 all-to-all-done.2
  30.4 4.6 all-to-all-start
  35.0 1.1 copy.199
  36.1 8.7 all-to-all-done
  44.8 4.8 all-to-all-start.1
  57.1 2.2 all-to-all-done.1
  59.3 1.7 conditional.13
  59.3 0.8 squeeze.147
  60.2 0.8 squeeze.146
  61.7 1.4 fusion.105
  63.1 3.3 conditional.9
  63.1 1.0 convolution_bitcast_fusion
  64.7 1.0 fusion
  67.8 108.2 %all-reduce.23.cloned.1.call-done = f32[1,128,128]{2,1,0:T(8,128)} async-done(((f32[1,128,128]{2,1,0:T(8,128)}), f32[1,128,128]{2,1,0:T(8,128)}) %all-reduce.23.cloned.1.call-update) | async-done | bytes 65552
  176.7 37.1 %all_gather.84 = f32[16,8,128]{2,1,0:T(8,128)S(1)} all-gather(f32[1,8,128]{2,1,0:T(8,128)S(1)} %constant_dynamic-slice_fusion.3), channel_id=1, replica_groups=mesh['node'=16,'slab'=16] {'node'}, dimensions={0}, use_global_device_ids=true | all-gather | bytes 69632 | tf_op jit(solution)/shard_map/all_gather | solution.py:101
  214.5 0.8 fusion.75
  215.3 25.6 %all-gather.5 = f32[128,128]{1,0:T(8,128)S(1)} all-gather(f32[8,128]{1,0:T(8,128)S(1)} %bitcast.485), channel_id=7, replica_groups=mesh['node'=16,'slab'=16] {'slab'}, dimensions={0}, use_global_device_ids=true | all-gather | bytes 69632 | tf_op jit(solution)/shard_map/all_gather | solution.py:106
  240.9 18.1 %all-gather.4 = f32[128,128]{1,0:T(8,128)S(1)} all-gather(f32[8,128]{1,0:T(8,128)S(1)} %bitcast.484), channel_id=6, replica_groups=mesh['node'=16,'slab'=16] {'slab'}, dimensions={0}, use_global_device_ids=true | all-gather | bytes 69632 | tf_op jit(solution)/shard_map/all_gather | solution.py:105
  263.6 106.7 %all-reduce.31.cloned.1.call-done = (f32[1,128,128]{2,1,0:T(8,128)}, f32[1,128,128]{2,0,1:T(1,128)}, f32[1,128,128]{2,0,1:T(1,128)}) async-done(((f32[1,128,128]{2,1,0:T(8,128)}, f32[1,128,128]{2,0,1:T(1,128)}, f32[1,128,128]{2,0,1:T(1,128)}), (f32[1,128,128]{2,1,0:T(8,128)}, f32[1,128,128]{2,0,1:T(1,128)}, f32[1,128,128]{2,0,1:T(1,128)})) %all-reduce.31.cloned.1.call-update) | async-done | bytes 196624
  370.9 37.4 %all_gather.87 = f32[16,8,128]{2,1,0:T(8,128)S(1)} all-gather(f32[1,8,128]{2,1,0:T(8,128)S(1)} %constant_dynamic-slice_fusion.2), channel_id=1, replica_groups=mesh['node'=16,'slab'=16] {'node'}, dimensions={0}, use_global_device_ids=true | all-gather | bytes 69632 | tf_op jit(solution)/shard_map/all_gather | solution.py:101
  409.1 0.8 fusion.71
  411.3 24.4 %all-gather.7 = f32[128,128]{1,0:T(8,128)S(1)} all-gather(f32[8,128]{1,0:T(8,128)S(1)} %bitcast.477), channel_id=9, replica_groups=mesh['node'=16,'slab'=16] {'slab'}, dimensions={0}, use_global_device_ids=true | all-gather | bytes 69632 | tf_op jit(solution)/shard_map/all_gather | solution.py:106
  435.7 18.1 %all-gather.6 = f32[128,128]{1,0:T(8,128)S(1)} all-gather(f32[8,128]{1,0:T(8,128)S(1)} %bitcast.475), channel_id=8, replica_groups=mesh['node'=16,'slab'=16] {'slab'}, dimensions={0}, use_global_device_ids=true | all-gather | bytes 69632 | tf_op jit(solution)/shard_map/all_gather | solution.py:105
  453.8 31.3 %all_gather.73 = f32[16,8,128]{2,1,0:T(8,128)S(1)} all-gather(f32[1,8,128]{2,1,0:T(8,128)S(1)} %bitcast.492), channel_id=1, replica_groups=mesh['node'=16,'slab'=16] {'node'}, dimensions={0}, use_global_device_ids=true | all-gather | bytes 69632 | tf_op jit(solution)/shard_map/all_gather | solution.py:145
  485.2 0.8 fusion.57
  485.9 33.3 %all_gather.72 = f32[16,8,128]{2,1,0:T(8,128)S(1)} all-gather(f32[1,8,128]{2,1,0:T(8,128)S(1)} %bitcast.489), channel_id=1, replica_groups=mesh['node'=16,'slab'=16] {'node'}, dimensions={0}, use_global_device_ids=true | all-gather | bytes 69632 | tf_op jit(solution)/shard_map/all_gather | solution.py:144
  519.2 0.8 fusion.59
  520.0 30.2 %all-gather = f32[128,128]{1,0:T(8,128)S(1)} all-gather(f32[8,128]{1,0:T(8,128)S(1)} %broadcast_select_fusion.4), channel_id=2, replica_groups=mesh['node'=16,'slab'=16] {'slab'}, dimensions={0}, use_global_device_ids=true | all-gather | bytes 69632 | tf_op jit(solution)/shard_map/all_gather | solution.py:150
  552.5 112.1 %all-reduce.29.cloned.1.call-done = (f32[1,128,128]{2,1,0:T(8,128)}, f32[1,128,128]{2,0,1:T(1,128)}, f32[1,128,128]{2,0,1:T(1,128)}) async-done(((f32[1,128,128]{2,1,0:T(8,128)}, f32[1,128,128]{2,0,1:T(1,128)}, f32[1,128,128]{2,0,1:T(1,128)}), (f32[1,128,128]{2,1,0:T(8,128)}, f32[1,128,128]{2,0,1:T(1,128)}, f32[1,128,128]{2,0,1:T(1,128)})) %all-reduce.29.cloned.1.call-update) | async-done | bytes 196624
  665.3 37.4 %all_gather.90 = f32[16,8,128]{2,1,0:T(8,128)S(1)} all-gather(f32[1,8,128]{2,1,0:T(8,128)S(1)} %constant_dynamic-slice_fusion.1), channel_id=1, replica_groups=mesh['node'=16,'slab'=16] {'node'}, dimensions={0}, use_global_device_ids=true | all-gather | bytes 69632 | tf_op jit(solution)/shard_map/all_gather | solution.py:101
  703.4 0.8 fusion.67
  705.7 24.4 %all-gather.9 = f32[128,128]{1,0:T(8,128)S(1)} all-gather(f32[8,128]{1,0:T(8,128)S(1)} %bitcast.478), channel_id=11, replica_groups=mesh['node'=16,'slab'=16] {'slab'}, dimensions={0}, use_global_device_ids=true | all-gather | bytes 69632 | tf_op jit(solution)/shard_map/all_gather | solution.py:106
  730.0 18.1 %all-gather.8 = f32[128,128]{1,0:T(8,128)S(1)} all-gather(f32[8,128]{1,0:T(8,128)S(1)} %bitcast.476), channel_id=10, replica_groups=mesh['node'=16,'slab'=16] {'slab'}, dimensions={0}, use_global_device_ids=true | all-gather | bytes 69632 | tf_op jit(solution)/shard_map/all_gather | solution.py:105
  748.2 31.3 %all_gather.76 = f32[16,8,128]{2,1,0:T(8,128)S(1)} all-gather(f32[1,8,128]{2,1,0:T(8,128)S(1)} %bitcast.493), channel_id=1, replica_groups=mesh['node'=16,'slab'=16] {'node'}, dimensions={0}, use_global_device_ids=true | all-gather | bytes 69632 | tf_op jit(solution)/shard_map/all_gather | solution.py:145
  779.5 0.8 fusion.53
  780.3 33.3 %all_gather.75 = f32[16,8,128]{2,1,0:T(8,128)S(1)} all-gather(f32[1,8,128]{2,1,0:T(8,128)S(1)} %bitcast.490), channel_id=1, replica_groups=mesh['node'=16,'slab'=16] {'node'}, dimensions={0}, use_global_device_ids=true | all-gather | bytes 69632 | tf_op jit(solution)/shard_map/all_gather | solution.py:144
  814.4 30.2 %all-gather.1 = f32[128,128]{1,0:T(8,128)S(1)} all-gather(f32[8,128]{1,0:T(8,128)S(1)} %broadcast_select_fusion.3), channel_id=3, replica_groups=mesh['node'=16,'slab'=16] {'slab'}, dimensions={0}, use_global_device_ids=true | all-gather | bytes 69632 | tf_op jit(solution)/shard_map/all_gather | solution.py:150
  847.0 113.2 %all-reduce.27.cloned.1.call-done = (f32[1,128,128]{2,1,0:T(8,128)}, f32[1,128,128]{2,0,1:T(1,128)}, f32[1,128,128]{2,0,1:T(1,128)}) async-done(((f32[1,128,128]{2,1,0:T(8,128)}, f32[1,128,128]{2,0,1:T(1,128)}, f32[1,128,128]{2,0,1:T(1,128)}), (f32[1,128,128]{2,1,0:T(8,128)}, f32[1,128,128]{2,0,1:T(1,128)}, f32[1,128,128]{2,0,1:T(1,128)})) %all-reduce.27.cloned.1.call-update) | async-done | bytes 196624
  960.9 37.4 %all_gather.93 = f32[16,8,128]{2,1,0:T(8,128)S(1)} all-gather(f32[1,8,128]{2,1,0:T(8,128)S(1)} %constant_dynamic-slice_fusion), channel_id=1, replica_groups=mesh['node'=16,'slab'=16] {'node'}, dimensions={0}, use_global_device_ids=true | all-gather | bytes 69632 | tf_op jit(solution)/shard_map/all_gather | solution.py:101
  999.0 0.8 fusion.63
  1001.2 24.3 %all-gather.11 = f32[128,128]{1,0:T(8,128)S(1)} all-gather(f32[8,128]{1,0:T(8,128)S(1)} %bitcast.473), channel_id=13, replica_groups=mesh['node'=16,'slab'=16] {'slab'}, dimensions={0}, use_global_device_ids=true | all-gather | bytes 69632 | tf_op jit(solution)/shard_map/all_gather | solution.py:106
  1025.6 18.1 %all-gather.10 = f32[128,128]{1,0:T(8,128)S(1)} all-gather(f32[8,128]{1,0:T(8,128)S(1)} %bitcast.474), channel_id=12, replica_groups=mesh['node'=16,'slab'=16] {'slab'}, dimensions={0}, use_global_device_ids=true | all-gather | bytes 69632 | tf_op jit(solution)/shard_map/all_gather | solution.py:105
  1043.7 31.3 %all_gather.79 = f32[16,8,128]{2,1,0:T(8,128)S(1)} all-gather(f32[1,8,128]{2,1,0:T(8,128)S(1)} %bitcast.494), channel_id=1, replica_groups=mesh['node'=16,'slab'=16] {'node'}, dimensions={0}, use_global_device_ids=true | all-gather | bytes 69632 | tf_op jit(solution)/shard_map/all_gather | solution.py:145
  1075.8 33.3 %all_gather.78 = f32[16,8,128]{2,1,0:T(8,128)S(1)} all-gather(f32[1,8,128]{2,1,0:T(8,128)S(1)} %bitcast.491), channel_id=1, replica_groups=mesh['node'=16,'slab'=16] {'node'}, dimensions={0}, use_global_device_ids=true | all-gather | bytes 69632 | tf_op jit(solution)/shard_map/all_gather | solution.py:144
  1109.9 30.2 %all-gather.2 = f32[128,128]{1,0:T(8,128)S(1)} all-gather(f32[8,128]{1,0:T(8,128)S(1)} %broadcast_select_fusion.2), channel_id=4, replica_groups=mesh['node'=16,'slab'=16] {'slab'}, dimensions={0}, use_global_device_ids=true | all-gather | bytes 69632 | tf_op jit(solution)/shard_map/all_gather | solution.py:150
  1141.6 6.6 conditional.17
  1143.5 1.0 convolution_bitcast_fusion.22
  1144.7 1.4 convolution_bitcast_fusion.21
  1146.1 2.1 fusion.29
  1149.5 108.8 %all-reduce.25.cloned.1.call-done = (f32[1,128,128]{2,0,1:T(1,128)}, f32[1,128,128]{2,0,1:T(1,128)}, f32[1,128,128]{2,1,0:T(8,128)}) async-done(((f32[1,128,128]{2,0,1:T(1,128)}, f32[1,128,128]{2,0,1:T(1,128)}, f32[1,128,128]{2,1,0:T(8,128)}), (f32[1,128,128]{2,0,1:T(1,128)}, f32[1,128,128]{2,0,1:T(1,128)}, f32[1,128,128]{2,1,0:T(8,128)})) %all-reduce.25.cloned.1.call-update) | async-done | bytes 196624
  1259.6 37.4 %all_gather.81 = f32[16,8,128]{2,1,0:T(8,128)S(1)} all-gather(f32[1,8,128]{2,1,0:T(8,128)S(1)} %bitcast.496), channel_id=1, replica_groups=mesh['node'=16,'slab'=16] {'node'}, dimensions={0}, use_global_device_ids=true | all-gather | bytes 69632 | tf_op jit(solution)/shard_map/all_gather | solution.py:144
  1297.8 31.3 %all_gather.82 = f32[16,8,128]{2,1,0:T(8,128)S(1)} all-gather(f32[1,8,128]{2,1,0:T(8,128)S(1)} %bitcast.495), channel_id=1, replica_groups=mesh['node'=16,'slab'=16] {'node'}, dimensions={0}, use_global_device_ids=true | all-gather | bytes 69632 | tf_op jit(solution)/shard_map/all_gather | solution.py:145
  1329.9 31.3 %all-gather.3 = f32[128,128]{1,0:T(8,128)S(1)} all-gather(f32[8,128]{1,0:T(8,128)S(1)} %broadcast_select_fusion.1), channel_id=5, replica_groups=mesh['node'=16,'slab'=16] {'slab'}, dimensions={0}, use_global_device_ids=true | all-gather | bytes 69632 | tf_op jit(solution)/shard_map/all_gather | solution.py:150
  1361.2 1.6 convolution_bitcast_fusion.24
  1362.9 1.1 copy.233
  1364.0 3.5 all-to-all-start.3
  1367.5 1.3 fusion.78
  1369.4 75.3 %psum.7 = f32[]{:T(128)} all-reduce(f32[]{:T(128)S(6)} %select_n.174), channel_id=1, replica_groups=mesh['node'=16,'slab'=16] {'node','slab'}, use_global_device_ids=true, to_apply=%region_43.44 | all-reduce | flops 1 | bytes 8 | tf_op jit(solution)/shard_map/psum | solution.py:116
  1445.7 1.1 copy.237
  (123 shorter events, 34.4 us)
Async XLA Ops:
  7.2 1.4 copy-start
  7.2 0.7 copy-start.15
  8.6 2.7 copy-start.6
  13.5 16.8 %all-to-all-start.2 = ((f32[1,8,128,128]{3,1,0,2:T(8,128)}), f32[1,8,128,128]{3,1,0,2:T(8,128)S(1)}, u32[]{:S(2)}, u32[]{:S(2)}) async-start(f32[1,8,128,128]{3,1,0,2:T(8,128)} %copy.218), calls=%async_computation.2 | async-start | bytes 1048576 | tf_op jit(solution)/shard_map/all_to_all | solution.py:55
  30.4 14.4 all-to-all-start
  44.7 7.4 copy-start.16
  44.7 10.2 copy-start.17
  44.8 14.5 all-to-all-start.1
  49.5 7.3 copy-start.9
  49.5 126.5 %all-reduce.23.cloned.1.call-start = ((), (), s32[]{:S(2)}) async-start(), calls=%async_computation.4 | async-start | bytes 131072
  61.0 0.6 copy-start.14
  61.7 308.6 %all-reduce.31.cloned.1.call-start = ((), (), s32[]{:S(2)}) async-start(), calls=%async_computation.8 | async-start | bytes 393216
  259.6 0.6 copy-start.11
  260.3 404.3 %all-reduce.29.cloned.1.call-start = ((), (), s32[]{:S(2)}) async-start(), calls=%async_computation.7 | async-start | bytes 393216
  551.8 0.6 copy-start.12
  552.4 407.7 %all-reduce.27.cloned.1.call-start = ((), (), s32[]{:S(2)}) async-start(), calls=%async_computation.6 | async-start | bytes 393216
  846.3 0.6 copy-start.13
  847.0 411.3 %all-reduce.25.cloned.1.call-start = ((), (), s32[]{:S(2)}) async-start(), calls=%async_computation.5 | async-start | bytes 393216
  1140.1 1.5 copy-start.5
  1143.5 1.0 copy-start.7
  1146.1 2.1 copy-start.8
  1148.2 0.6 copy-start.10
  1364.0 80.8 %all-to-all-start.3 = ((f32[1,8,128,128]{2,1,0,3:T(8,128)}), f32[1,8,128,128]{2,1,0,3:T(8,128)S(1)}, u32[]{:S(2)}, u32[]{:S(2)}) async-start(f32[1,8,128,128]{2,1,0,3:T(8,128)} %copy.233), calls=%async_computation.3 | async-start | bytes 1048576 | tf_op jit(solution)/shard_map/all_to_all | solution.py:155
Sparse Core Ops, SparseCore 0:
  61.8 114.1 all-reduce.22
  260.4 109.8 all-reduce.30
  552.6 111.9 all-reduce.28
  847.1 113.0 all-reduce.26
  1149.0 109.2 all-reduce.24
where the time goes:
time: 1460 us; the launch traced here: 1450 us
  blocking collectives  780 us (53%)
  waiting for transfers between devices  569 us (39%)
  matrix products  27.1 us (2%)
  local copies, waits for them, and re-layouts  26.8 us (2%)
  between operations  23.6 us (2%)
  starting transfers between devices  20.3 us (1%)
    unnamed x10, waiting for transfers between devices  549 us
    all_gather x4, blocking collectives, per_device(): every_rows = lax.all_gather(up_rows, 'node', axis=0, tiled=True)  149 us
    all_gather x4, blocking collectives, per_device(): lax.all_gather(rows_left, 'node', axis=0, tiled=True)  137 us
    all_gather x4, blocking collectives, per_device(): lax.all_gather(rows_right, 'node', axis=0, tiled=True)  125 us
    all_gather x4, blocking collectives, per_device(): full_down = lax.all_gather(mine, 'slab', axis=1, tiled=True)  122 us
    all_gather x4, blocking collectives, per_device(): lax.all_gather(right_rows, 'slab', axis=1, tiled=True)  98.7 us
    psum x1, blocking collectives, per_device(): energy = lax.psum(jnp.sum(own), ('node', 'slab'))  75.3 us
    all_gather x4, blocking collectives, per_device(): lax.all_gather(left_rows, 'slab', axis=1, tiled=True)  72.6 us
  transfers between devices with their start and end apart: 9, of which 8 were waited for; matrix products, arithmetic and copies ran while one was open for 1% of the time, Pallas kernels for 0%

commit v1 on v0

--- a/solution.py
+++ b/solution.py
@@ -141,7 +141,9 @@
             lax.psum_scatter(part_right, "slab", scatter_dimension=1, tiled=True),
         )
         every_left, every_right = (
-            lax.all_gather(rows_left, "node", axis=0, tiled=True),
+            jnp.concatenate(
+                lax.all_to_all(jnp.stack([rows_left] * lax.axis_size("node")), "node", 0, 0), axis=0
+            ),
             lax.all_gather(rows_right, "node", axis=0, tiled=True),
         )
         from_left = select_rows(onehot_parent, every_left)

time: 1460 us -> 1350 us (0.925)
  blocking collectives: 780 us -> 625 us
  waiting for transfers between devices: 569 us -> 592 us
  starting transfers between devices: 20.3 us -> 42.1 us
    all_gather x4 -> x0, blocking collectives: 137 us -> none  [per_device(): lax.all_gather(rows_left, 'node', axis=0, tiled=True)]
    all_gather x4, blocking collectives: 122 us -> 99.7 us  [per_device(): full_down = lax.all_gather(mine, 'slab', axis=1, tiled=True)]
    all_to_all x0 -> x4, starting transfers between devices: none -> 21.8 us  [per_device(): lax.all_to_all(jnp.stack([rows_left] * lax.axis_size('node')), 'node', 0, 0)]
    all_to_all x0 -> x4, waiting for transfers between devices: none -> 17.5 us  [per_device(): lax.all_to_all(jnp.stack([rows_left] * lax.axis_size('node')), 'node', 0, 0)]
  transfers between devices with their start and end apart: 9 -> 13, of which waited for: 8 -> 11; matrix products, arithmetic and copies ran while one was open for 1% -> 2% of each run, Pallas kernels for 0% -> 0%
where the time goes in v1:
time: 1350 us; the launch traced here: 1340 us
  blocking collectives  625 us (46%)
  waiting for transfers between devices  592 us (44%)
  starting transfers between devices  42.1 us (3%)
  local copies, waits for them, and re-layouts  27.5 us (2%)
  matrix products  26.6 us (2%)
  between operations  23.6 us (2%)
    unnamed x10, waiting for transfers between devices  555 us
    all_gather x4, blocking collectives, per_device(): every_rows = lax.all_gather(up_rows, 'node', axis=0, tiled=True)  149 us
    all_gather x4, blocking collectives, per_device(): lax.all_gather(rows_right, 'node', axis=0, tiled=True)  131 us
    all_gather x4, blocking collectives, per_device(): full_down = lax.all_gather(mine, 'slab', axis=1, tiled=True)  99.7 us
    all_gather x4, blocking collectives, per_device(): lax.all_gather(right_rows, 'slab', axis=1, tiled=True)  98.6 us
    psum x1, blocking collectives, per_device(): energy = lax.psum(jnp.sum(own), ('node', 'slab'))  74.1 us
    all_gather x4, blocking collectives, per_device(): lax.all_gather(left_rows, 'slab', axis=1, tiled=True)  72.6 us
  transfers between devices with their start and end apart: 13, of which 11 were waited for; matrix products, arithmetic and copies ran while one was open for 2% of the time, Pallas kernels for 0%

profile of v1, /device:TPU:1, one launch (start us, length us, event | category | flops | bytes accessed | tf_op | source)
XLA Modules:
  0.0 1344.1 jit_solution(9218602184468659610)
XLA Ops:
  8.6 1.4 fusion.39
  9.9 1.3 fusion.41
  12.4 1.1 copy.218
  13.6 7.2 all-to-all-start.6
  20.7 1.0 copy.201
  21.7 8.7 all-to-all-done.6
  30.4 4.6 all-to-all-start
  35.0 1.1 copy.203
  36.1 8.6 all-to-all-done
  44.8 4.8 all-to-all-start.1
  57.1 2.2 all-to-all-done.1
  59.3 1.7 conditional.13
  59.3 0.9 squeeze.147
  60.2 0.8 squeeze.146
  61.7 1.3 fusion.105
  63.1 3.3 conditional.9
  63.1 1.0 convolution_bitcast_fusion
  64.7 1.0 fusion
  67.8 108.3 %all-reduce.23.cloned.1.call-done = f32[1,128,128]{2,1,0:T(8,128)} async-done(((f32[1,128,128]{2,1,0:T(8,128)}), f32[1,128,128]{2,1,0:T(8,128)}) %all-reduce.23.cloned.1.call-update) | async-done | bytes 65552
  176.9 37.1 %all_gather.68 = f32[16,8,128]{2,1,0:T(8,128)S(1)} all-gather(f32[1,8,128]{2,1,0:T(8,128)S(1)} %constant_dynamic-slice_fusion.3), channel_id=1, replica_groups=mesh['node'=16,'slab'=16] {'node'}, dimensions={0}, use_global_device_ids=true | all-gather | bytes 69632 | tf_op jit(solution)/shard_map/all_gather | solution.py:101
  215.4 25.6 %all-gather.5 = f32[128,128]{1,0:T(8,128)S(1)} all-gather(f32[8,128]{1,0:T(8,128)S(1)} %bitcast.495), channel_id=7, replica_groups=mesh['node'=16,'slab'=16] {'slab'}, dimensions={0}, use_global_device_ids=true | all-gather | bytes 69632 | tf_op jit(solution)/shard_map/all_gather | solution.py:106
  241.0 18.1 %all-gather.4 = f32[128,128]{1,0:T(8,128)S(1)} all-gather(f32[8,128]{1,0:T(8,128)S(1)} %bitcast.494), channel_id=6, replica_groups=mesh['node'=16,'slab'=16] {'slab'}, dimensions={0}, use_global_device_ids=true | all-gather | bytes 69632 | tf_op jit(solution)/shard_map/all_gather | solution.py:105
  263.6 106.8 %all-reduce.31.cloned.1.call-done = (f32[1,128,128]{2,1,0:T(8,128)}, f32[1,128,128]{2,0,1:T(1,128)}, f32[1,128,128]{2,0,1:T(1,128)}) async-done(((f32[1,128,128]{2,1,0:T(8,128)}, f32[1,128,128]{2,0,1:T(1,128)}, f32[1,128,128]{2,0,1:T(1,128)}), (f32[1,128,128]{2,1,0:T(8,128)}, f32[1,128,128]{2,0,1:T(1,128)}, f32[1,128,128]{2,0,1:T(1,128)})) %all-reduce.31.cloned.1.call-update) | async-done | bytes 196624
  371.0 37.4 %all_gather.71 = f32[16,8,128]{2,1,0:T(8,128)S(1)} all-gather(f32[1,8,128]{2,1,0:T(8,128)S(1)} %constant_dynamic-slice_fusion.2), channel_id=1, replica_groups=mesh['node'=16,'slab'=16] {'node'}, dimensions={0}, use_global_device_ids=true | all-gather | bytes 69632 | tf_op jit(solution)/shard_map/all_gather | solution.py:101
  411.2 24.3 %all-gather.7 = f32[128,128]{1,0:T(8,128)S(1)} all-gather(f32[8,128]{1,0:T(8,128)S(1)} %bitcast.491), channel_id=9, replica_groups=mesh['node'=16,'slab'=16] {'slab'}, dimensions={0}, use_global_device_ids=true | all-gather | bytes 69632 | tf_op jit(solution)/shard_map/all_gather | solution.py:106
  435.6 18.1 %all-gather.6 = f32[128,128]{1,0:T(8,128)S(1)} all-gather(f32[8,128]{1,0:T(8,128)S(1)} %bitcast.486), channel_id=8, replica_groups=mesh['node'=16,'slab'=16] {'slab'}, dimensions={0}, use_global_device_ids=true | all-gather | bytes 69632 | tf_op jit(solution)/shard_map/all_gather | solution.py:105
  453.7 31.3 %all_gather.60 = f32[16,8,128]{2,1,0:T(8,128)S(1)} all-gather(f32[1,8,128]{2,1,0:T(8,128)S(1)} %bitcast.503), channel_id=1, replica_groups=mesh['node'=16,'slab'=16] {'node'}, dimensions={0}, use_global_device_ids=true | all-gather | bytes 69632 | tf_op jit(solution)/shard_map/all_gather | solution.py:147
  485.7 4.2 all-to-all-start.2
  490.1 0.8 fusion.57
  490.8 8.0 all-to-all-done.2
  499.7 24.9 %all-gather = f32[128,128]{1,0:T(8,128)S(1)} all-gather(f32[8,128]{1,0:T(8,128)S(1)} %broadcast_select_fusion.4), channel_id=2, replica_groups=mesh['node'=16,'slab'=16] {'slab'}, dimensions={0}, use_global_device_ids=true | all-gather | bytes 69632 | tf_op jit(solution)/shard_map/all_gather | solution.py:152
  526.1 112.9 %all-reduce.29.cloned.1.call-done = (f32[1,128,128]{2,1,0:T(8,128)}, f32[1,128,128]{2,0,1:T(1,128)}, f32[1,128,128]{2,0,1:T(1,128)}) async-done(((f32[1,128,128]{2,1,0:T(8,128)}, f32[1,128,128]{2,0,1:T(1,128)}, f32[1,128,128]{2,0,1:T(1,128)}), (f32[1,128,128]{2,1,0:T(8,128)}, f32[1,128,128]{2,0,1:T(1,128)}, f32[1,128,128]{2,0,1:T(1,128)})) %all-reduce.29.cloned.1.call-update) | async-done | bytes 196624
  639.6 37.4 %all_gather.74 = f32[16,8,128]{2,1,0:T(8,128)S(1)} all-gather(f32[1,8,128]{2,1,0:T(8,128)S(1)} %constant_dynamic-slice_fusion.1), channel_id=1, replica_groups=mesh['node'=16,'slab'=16] {'node'}, dimensions={0}, use_global_device_ids=true | all-gather | bytes 69632 | tf_op jit(solution)/shard_map/all_gather | solution.py:101
  679.9 24.3 %all-gather.9 = f32[128,128]{1,0:T(8,128)S(1)} all-gather(f32[8,128]{1,0:T(8,128)S(1)} %bitcast.492), channel_id=11, replica_groups=mesh['node'=16,'slab'=16] {'slab'}, dimensions={0}, use_global_device_ids=true | all-gather | bytes 69632 | tf_op jit(solution)/shard_map/all_gather | solution.py:106
  704.2 18.1 %all-gather.8 = f32[128,128]{1,0:T(8,128)S(1)} all-gather(f32[8,128]{1,0:T(8,128)S(1)} %bitcast.488), channel_id=10, replica_groups=mesh['node'=16,'slab'=16] {'slab'}, dimensions={0}, use_global_device_ids=true | all-gather | bytes 69632 | tf_op jit(solution)/shard_map/all_gather | solution.py:105
  722.3 31.3 %all_gather.62 = f32[16,8,128]{2,1,0:T(8,128)S(1)} all-gather(f32[1,8,128]{2,1,0:T(8,128)S(1)} %bitcast.504), channel_id=1, replica_groups=mesh['node'=16,'slab'=16] {'node'}, dimensions={0}, use_global_device_ids=true | all-gather | bytes 69632 | tf_op jit(solution)/shard_map/all_gather | solution.py:147
  754.3 4.3 all-to-all-start.3
  758.9 0.8 fusion.53
  759.7 7.8 all-to-all-done.3
  768.3 24.9 %all-gather.1 = f32[128,128]{1,0:T(8,128)S(1)} all-gather(f32[8,128]{1,0:T(8,128)S(1)} %broadcast_select_fusion.3), channel_id=3, replica_groups=mesh['node'=16,'slab'=16] {'slab'}, dimensions={0}, use_global_device_ids=true | all-gather | bytes 69632 | tf_op jit(solution)/shard_map/all_gather | solution.py:152
  794.7 113.8 %all-reduce.27.cloned.1.call-done = (f32[1,128,128]{2,1,0:T(8,128)}, f32[1,128,128]{2,0,1:T(1,128)}, f32[1,128,128]{2,0,1:T(1,128)}) async-done(((f32[1,128,128]{2,1,0:T(8,128)}, f32[1,128,128]{2,0,1:T(1,128)}, f32[1,128,128]{2,0,1:T(1,128)}), (f32[1,128,128]{2,1,0:T(8,128)}, f32[1,128,128]{2,0,1:T(1,128)}, f32[1,128,128]{2,0,1:T(1,128)})) %all-reduce.27.cloned.1.call-update) | async-done | bytes 196624
  909.2 37.4 %all_gather.77 = f32[16,8,128]{2,1,0:T(8,128)S(1)} all-gather(f32[1,8,128]{2,1,0:T(8,128)S(1)} %constant_dynamic-slice_fusion), channel_id=1, replica_groups=mesh['node'=16,'slab'=16] {'node'}, dimensions={0}, use_global_device_ids=true | all-gather | bytes 69632 | tf_op jit(solution)/shard_map/all_gather | solution.py:101
  949.4 24.3 %all-gather.11 = f32[128,128]{1,0:T(8,128)S(1)} all-gather(f32[8,128]{1,0:T(8,128)S(1)} %bitcast.484), channel_id=13, replica_groups=mesh['node'=16,'slab'=16] {'slab'}, dimensions={0}, use_global_device_ids=true | all-gather | bytes 69632 | tf_op jit(solution)/shard_map/all_gather | solution.py:106
  973.8 18.1 %all-gather.10 = f32[128,128]{1,0:T(8,128)S(1)} all-gather(f32[8,128]{1,0:T(8,128)S(1)} %bitcast.485), channel_id=12, replica_groups=mesh['node'=16,'slab'=16] {'slab'}, dimensions={0}, use_global_device_ids=true | all-gather | bytes 69632 | tf_op jit(solution)/shard_map/all_gather | solution.py:105
  991.9 31.3 %all_gather.64 = f32[16,8,128]{2,1,0:T(8,128)S(1)} all-gather(f32[1,8,128]{2,1,0:T(8,128)S(1)} %bitcast.505), channel_id=1, replica_groups=mesh['node'=16,'slab'=16] {'node'}, dimensions={0}, use_global_device_ids=true | all-gather | bytes 69632 | tf_op jit(solution)/shard_map/all_gather | solution.py:147
  1023.9 4.2 all-to-all-start.4
  1028.2 6.4 conditional.17
  1029.9 1.0 convolution_bitcast_fusion.22
  1031.1 1.4 convolution_bitcast_fusion.21
  1032.5 2.1 fusion.29
  1034.7 0.8 fusion.49
  1035.4 1.6 all-to-all-done.4
  1037.9 24.9 %all-gather.2 = f32[128,128]{1,0:T(8,128)S(1)} all-gather(f32[8,128]{1,0:T(8,128)S(1)} %broadcast_select_fusion.2), channel_id=4, replica_groups=mesh['node'=16,'slab'=16] {'slab'}, dimensions={0}, use_global_device_ids=true | all-gather | bytes 69632 | tf_op jit(solution)/shard_map/all_gather | solution.py:152
  1065.1 113.1 %all-reduce.25.cloned.1.call-done = (f32[1,128,128]{2,0,1:T(1,128)}, f32[1,128,128]{2,0,1:T(1,128)}, f32[1,128,128]{2,1,0:T(8,128)}) async-done(((f32[1,128,128]{2,0,1:T(1,128)}, f32[1,128,128]{2,0,1:T(1,128)}, f32[1,128,128]{2,1,0:T(8,128)}), (f32[1,128,128]{2,0,1:T(1,128)}, f32[1,128,128]{2,0,1:T(1,128)}, f32[1,128,128]{2,1,0:T(8,128)})) %all-reduce.25.cloned.1.call-update) | async-done | bytes 196624
  1180.2 9.0 all-to-all-start.5
  1189.2 36.9 %all_gather.66 = f32[16,8,128]{2,1,0:T(8,128)S(1)} all-gather(f32[1,8,128]{2,1,0:T(8,128)S(1)} %bitcast.502), channel_id=1, replica_groups=mesh['node'=16,'slab'=16] {'node'}, dimensions={0}, use_global_device_ids=true | all-gather | bytes 69632 | tf_op jit(solution)/shard_map/all_gather | solution.py:147
  1227.0 0.8 fusion.47
  1227.8 25.1 %all-gather.3 = f32[128,128]{1,0:T(8,128)S(1)} all-gather(f32[8,128]{1,0:T(8,128)S(1)} %broadcast_select_fusion.1), channel_id=5, replica_groups=mesh['node'=16,'slab'=16] {'slab'}, dimensions={0}, use_global_device_ids=true | all-gather | bytes 69632 | tf_op jit(solution)/shard_map/all_gather | solution.py:152
  1252.9 1.6 convolution_bitcast_fusion.24
  1254.5 1.1 copy.233
  1255.6 3.5 all-to-all-start.7
  1259.2 1.3 fusion.78
  1261.1 74.1 %psum.7 = f32[]{:T(128)} all-reduce(f32[]{:T(128)S(6)} %select_n.174), channel_id=1, replica_groups=mesh['node'=16,'slab'=16] {'node','slab'}, use_global_device_ids=true, to_apply=%region_43.44 | all-reduce | flops 1 | bytes 8 | tf_op jit(solution)/shard_map/psum | solution.py:116
  1336.2 1.1 copy.237
  (131 shorter events, 37.3 us)
Async XLA Ops:
  7.2 1.4 copy-start
  7.2 0.7 copy-start.15
  8.6 2.7 copy-start.6
  13.6 16.8 %all-to-all-start.6 = ((f32[1,8,128,128]{3,1,0,2:T(8,128)}), f32[1,8,128,128]{3,1,0,2:T(8,128)S(1)}, u32[]{:S(2)}, u32[]{:S(2)}) async-start(f32[1,8,128,128]{3,1,0,2:T(8,128)} %copy.218), calls=%async_computation.6 | async-start | bytes 1048576 | tf_op jit(solution)/shard_map/all_to_all | solution.py:55
  30.4 14.4 %all-to-all-start = ((f32[1,128,8,128]{3,2,0,1:T(8,128)}), f32[1,128,8,128]{3,2,0,1:T(8,128)S(1)}, u32[]{:S(2)}, u32[]{:S(2)}) async-start(f32[1,128,8,128]{3,2,0,1:T(8,128)} %bitcast.69), calls=%async_computation | async-start | bytes 1048576 | tf_op jit(solution)/shard_map/all_to_all | solution.py:50
  44.8 7.4 copy-start.16
  44.8 10.2 copy-start.17
  44.8 14.5 %all-to-all-start.1 = ((f32[1,8,128,128]{3,1,0,2:T(8,128)}), f32[1,8,128,128]{3,1,0,2:T(8,128)S(1)}, u32[]{:S(2)}, u32[]{:S(2)}) async-start(f32[1,8,128,128]{3,1,0,2:T(8,128)} %copy.203), calls=%async_computation.1 | async-start | bytes 1048576 | tf_op jit(solution)/shard_map/all_to_all | solution.py:54
  49.5 7.4 copy-start.9
  49.5 126.7 %all-reduce.23.cloned.1.call-start = ((), (), s32[]{:S(2)}) async-start(), calls=%async_computation.8 | async-start | bytes 131072
  61.0 0.6 copy-start.14
  61.7 308.7 %all-reduce.31.cloned.1.call-start = ((), (), s32[]{:S(2)}) async-start(), calls=%async_computation.12 | async-start | bytes 393216
  259.7 0.6 copy-start.11
  485.7 13.2 all-to-all-start.2
  489.9 149.0 %all-reduce.29.cloned.1.call-start = ((), (), s32[]{:S(2)}) async-start(), calls=%async_computation.11 | async-start | bytes 393216
  490.1 9.6 copy-start.12
  754.3 13.2 all-to-all-start.3
  758.6 150.0 %all-reduce.27.cloned.1.call-start = ((), (), s32[]{:S(2)}) async-start(), calls=%async_computation.10 | async-start | bytes 393216
  758.9 9.4 copy-start.13
  794.0 234.2 %copy-start.5 = (f32[128,8,128]{2,0,1:T(8,128)S(1)}, f32[128,8,128]{2,0,1:T(8,128)}, u32[]{:S(2)}) copy-start(f32[128,8,128]{2,0,1:T(8,128)} %get-tuple-element.477) | copy-start | bytes 1572868
  1023.9 13.2 all-to-all-start.4
  1028.1 150.1 %all-reduce.25.cloned.1.call-start = ((), (), s32[]{:S(2)}) async-start(), calls=%async_computation.9 | async-start | bytes 393216
  1029.9 1.0 copy-start.7
  1032.5 2.1 copy-start.8
  1034.6 3.2 copy-start.10
  1180.2 46.7 %all-to-all-start.5 = ((f32[16,1,8,128]{3,2,1,0:T(8,128)}), f32[16,1,8,128]{3,2,1,0:T(8,128)S(1)}, u32[]{:S(2)}, u32[]{:S(2)}) async-start(f32[16,1,8,128]{3,2,1,0:T(8,128)} %stack.11), calls=%async_computation.5 | async-start | bytes 131072 | tf_op jit(solution)/shard_map/all_to_all | solution.py:145
  1255.6 79.6 %all-to-all-start.7 = ((f32[1,8,128,128]{2,1,0,3:T(8,128)}), f32[1,8,128,128]{2,1,0,3:T(8,128)S(1)}, u32[]{:S(2)}, u32[]{:S(2)}) async-start(f32[1,8,128,128]{2,1,0,3:T(8,128)} %copy.233), calls=%async_computation.7 | async-start | bytes 1048576 | tf_op jit(solution)/shard_map/all_to_all | solution.py:157
Sparse Core Ops, SparseCore 0:
  61.8 114.3 all-reduce.22
  260.5 109.8 all-reduce.30
  526.2 112.7 all-reduce.28
  794.8 113.6 all-reduce.26
  1064.6 113.5 all-reduce.24
